TPU v7x, 32 devices: a whole 2x2x4 slice. The times are simulated.
32 devices in a mesh: cand: 16 (over z, x, core), tp: 2 (over y).
Axes of the slice: x: 2, y: 2, z: 4, core: 2. Of those that a mesh axis runs over, the one named last changes fastest.
Arguments:
- hidden_in: bfloat16 [128, 2, 8192], P('cand'), may hold values from -4 to 4
- queries: bfloat16 [128, 2, 32, 128], P('cand', None, 'tp'), may hold values from -128 to 128
- new_kv: bfloat16 [128, 2, 8, 2, 128], P('cand', None, 'tp'), may hold values from -5 to 5
- kv_cache: bfloat16 [128, 8, 2, 512, 128], P('cand', 'tp'), may hold values from -6 to 6
- lengths: int32 [128], P('cand'), may hold values from 128 to 512, as said below
- winner: int32 [8], replicated, may hold values from 0 to 15
- out_values: bfloat16 [4096, 8192], P('tp'), may hold values from -4 to 4
- out_scales: float32 [32, 64], P('tp'), may hold values from 0.008 to 0.032
Outputs:
- mixed: bfloat16 [128, 2, 8192], P('cand')
Inputs may be any that keep to these rules, and one draw needn't show every extreme that they name: `lengths`: every draw has some row with exactly 512 live slots.
All inputs are finite; a program needn't handle non-finite values.
Results may differ from a plain program's by a relative error of at most 0.013.
Values may be sent and summed in bfloat16 or wider, within the bound.
A program may use at most 128 MiB of HBM per device.

v0:
```python
import math

import jax
import jax.numpy as jnp
from jax import lax
from jax.sharding import PartitionSpec as P

BLOCK = 64
KB = 256


def own_blocks(cache_rows, row_lengths):

    def take_block(cache_row, row_length):
        return lax.dynamic_slice_in_dim(cache_row, row_length - BLOCK, BLOCK, 2)

    return jax.vmap(take_block)(cache_rows, row_lengths)


def local(hidden_in, queries, new_kv, kv_cache, lengths, winner, out_values, out_scales):
    problems = kv_cache.shape[0]
    kv_here = kv_cache.shape[1]
    steps_count = queries.shape[1]
    heads_here = queries.shape[2]
    head_dim = queries.shape[3]
    group = heads_here // kv_here
    blocks = own_blocks(kv_cache, lengths)
    owner_mask = winner == lax.axis_index("cand")
    masked = jnp.where(owner_mask[:, None, None, None, None], blocks, jnp.zeros((), jnp.bfloat16))
    forked = lax.psum(masked, "cand").astype(jnp.float32).astype(jnp.bfloat16)
    grouped = queries.reshape(problems, steps_count, kv_here, group, head_dim)
    factor = 1.0 / math.sqrt(head_dim)

    def scores_of(keys):
        return (
            jnp.einsum("ptkgd,pkjd->ptkgj", grouped, keys, preferred_element_type=jnp.float32)
            * factor
        )

    def combine_values(weights, values):
        return jnp.einsum("ptkgj,pkjd->ptkgd", weights, values, preferred_element_type=jnp.float32)

    fresh = jnp.transpose(new_kv, (0, 2, 3, 1, 4))
    fork_scores = scores_of(forked[:, :, 0])
    new_scores = scores_of(fresh[:, :, 0])
    causal = jnp.arange(steps_count)[None, :] <= jnp.arange(steps_count)[:, None]
    new_scores = jnp.where(causal[None, :, None, None, :], new_scores, -jnp.inf)
    live = lengths - BLOCK
    count = kv_cache.shape[3] // KB

    def block_scores(index):
        piece = lax.dynamic_slice_in_dim(kv_cache, index * KB, KB, 3)
        scores = scores_of(piece[:, :, 0])
        slots = index * KB + jnp.arange(KB, dtype=jnp.int32)
        valid = slots[None, :] < live[:, None]
        scores = jnp.where(valid[:, None, None, None, :], scores, -jnp.inf)
        return (scores, piece[:, :, 1])

    peak = jnp.maximum(jnp.max(fork_scores, -1), jnp.max(new_scores, -1))
    total = jnp.sum(jnp.exp(fork_scores - peak[..., None]), -1) + jnp.sum(
        jnp.exp(new_scores - peak[..., None]), -1
    )

    def first_pass(index, carry):
        peak_now, total_now = carry
        scores, unused_values = block_scores(index)
        higher = jnp.maximum(peak_now, jnp.max(scores, -1))
        total_now = total_now * jnp.exp(peak_now - higher) + jnp.sum(
            jnp.exp(scores - higher[..., None]), -1
        )
        return (higher, total_now)

    peak, total = lax.fori_loop(0, count, first_pass, (peak, total))

    def weigh(scores):
        return (jnp.exp(scores - peak[..., None]) / total[..., None]).astype(jnp.bfloat16)

    summed = combine_values(weigh(fork_scores), forked[:, :, 1]) + combine_values(
        weigh(new_scores), fresh[:, :, 1]
    )

    def second_pass(index, summed_now):
        scores, values = block_scores(index)
        return summed_now + combine_values(weigh(scores), values)

    summed = lax.fori_loop(0, count, second_pass, summed)
    attended = summed.astype(jnp.bfloat16).reshape(problems * steps_count, heads_here * head_dim)
    blocks_here = out_scales.shape[0]
    side = out_values.shape[0] // blocks_here
    width = out_values.shape[1]
    partial_terms = jnp.einsum(
        "rbk,bkn->rbn",
        attended.reshape(-1, blocks_here, side),
        out_values.reshape(blocks_here, side, width),
        preferred_element_type=jnp.float32,
    )
    spread = jnp.repeat(out_scales, side, axis=1)
    term = jnp.sum(partial_terms * spread[None], axis=1)
    residual = hidden_in.reshape(problems * steps_count, width)
    totals = lax.psum(term.astype(jnp.bfloat16), "tp").astype(jnp.float32)
    result = (residual.astype(jnp.float32) + totals).astype(jnp.bfloat16)
    return result.reshape(hidden_in.shape)


def solution(mesh):
    placed = (
        P("cand", None, None),
        P("cand", None, "tp", None),
        P("cand", None, "tp", None, None),
        P("cand", "tp", None, None, None),
        P("cand"),
        P(),
        P("tp", None),
        P("tp", None),
    )
    return jax.shard_map(
        local, mesh=mesh, in_specs=placed, out_specs=P("cand", None, None), check_vma=False
    )
```

profile of v0, /device:TPU:0, one launch (start us, length us, event | category | flops | bytes accessed | tf_op | source)
XLA Modules:
  0.0 181.5 jit_solution(16705224246081859264)
XLA Ops:
  6.5 0.0 all-reduce.3.cloned.1.call-start
  6.5 0.0 copy-start.6
  6.5 0.0 copy-start.5
  6.5 12.2 %copy.17 = bf16[8,4,2,512,128]{4,1,2,0,3:T(4,128)(2,1)} copy(bf16[8,4,2,512,128]{4,3,2,1,0:T(8,128)(2,1)} %param.15) | data formatting | bytes 16777216 | tf_op args[3]
  18.7 0.0 copy-done.6
  18.7 5.0 %gather_fusion = bf16[8,4,2,64,128]{4,1,2,3,0:T(4,128)(2,1)S(1)} fusion(bf16[8,4,2,512,128]{4,1,2,0,3:T(4,128)(2,1)} %copy.17, s32[8]{0:T(128)S(1)} %fusion.42), kind=kCustom, calls=%fused_computation | custom fusion | bytes 2097312 | tf_op jit(solution)/shard_map/vmap()/gather | solution.py:15
  23.7 0.0 copy-done.5
  23.8 1.1 copy_select_fusion
  24.9 0.0 all-reduce.3.cloned.1.call-update
  24.9 0.0 copy-start.1
  24.9 0.0 copy-start.2
  24.9 0.0 copy-start.3
  25.0 0.0 all-reduce.5.cloned.1.call-start
  25.0 7.6 %copy.22 = bf16[8,4,2,512,128]{4,3,1,0,2:T(8,128)(2,1)} copy(bf16[8,4,2,512,128]{4,3,2,1,0:T(8,128)(2,1)} %param.15) | data formatting | bytes 16777216 | tf_op jit(solution)/shard_map/while | solution.py:73
  32.6 0.0 copy-done.1
  32.6 0.0 copy-done.2
  32.7 0.0 copy-done.3
  32.7 0.2 broadcast_in_dim.120
  32.9 0.3 copy.44
  33.2 0.7 fusion.45
  33.9 87.6 %all-reduce.3.cloned.1.call-done = bf16[8,4,2,64,128]{4,3,1,0,2:T(8,128)(2,1)} async-done(((bf16[8,4,2,64,128]{4,3,1,0,2:T(8,128)(2,1)}), bf16[8,4,2,64,128]{4,3,1,0,2:T(8,128)(2,1)}) %all-reduce.3.cloned.1.call-update) | async-done | bytes 1048592 | tf_op jit(solution)/shard_map/psum | solution.py:30
  121.5 1.5 fusion.44
  123.1 0.3 exponential_reduce_fusion.1
  123.4 0.1 exponential_reduce_fusion.2
  123.5 0.0 copy-start.4
  123.5 5.8 %while.28 = (s32[]{:T(128)}, f32[8,2,4,4]{3,1,2,0:T(2,128)S(1)}, f32[8,2,4,4]{3,1,2,0:T(2,128)S(1)}, s32[8]{0:T(128)S(1)}, bf16[8,4,2,512,128]{4,3,1,0,2:T(8,128...) while((s32[]{:T(128)}, f32[8,2,4,4]{3,1,2,0:T(2,128)S(1)}, ...), condition=%wide.region_8.9_spmd, body=%wide.region_5.8_spmd.sunk | while | flops 17107716 | bytes 2706619 | solution.py:73
  123.6 0.1 broadcast_compare_fusion.5
  123.6 2.4 %fusion.55 = (f32[8,2,4,4]{3,1,2,0:T(2,128)S(1)}, f32[8,2,4,4,256]{4,3,1,2,0:T(4,128)S(1)}) fusion(bf16[8,2,4,4,128]{4,3,1,2,0:T(4,128)(2,1)S(1)} %get-tuple-element.409, bf16[8,4,2,512,128]{4,3,1,0,2:T(8,128)(2,1)} %get-tuple-element.408, s32[]{:T(128)S(6)} %select_n.75, pred[8,256]{1,0:T(8,128)(4,1)S(1)} %broadcast_compare_fusion.5), kind=kOutput, calls=%fused_computation.71.clone.1 | convolution fusion | flops 16973568 | bytes 2427908 | tf_op jit(solution)/shard_map/while/body/eval_jaxpr/ptkgd,pkjd->ptkgj/dot_general | solution.py:36
  126.1 0.3 exponential_reduce_fusion.4
  126.5 0.1 broadcast_compare_fusion.5
  126.5 2.4 %fusion.55 = (f32[8,2,4,4]{3,1,2,0:T(2,128)S(1)}, f32[8,2,4,4,256]{4,3,1,2,0:T(4,128)S(1)}) fusion(bf16[8,2,4,4,128]{4,3,1,2,0:T(4,128)(2,1)S(1)} %get-tuple-element.409, bf16[8,4,2,512,128]{4,3,1,0,2:T(8,128)(2,1)} %get-tuple-element.408, s32[]{:T(128)S(6)} %select_n.75, pred[8,256]{1,0:T(8,128)(4,1)S(1)} %broadcast_compare_fusion.5), kind=kOutput, calls=%fused_computation.71.clone.1 | convolution fusion | flops 16973568 | bytes 2427908 | tf_op jit(solution)/shard_map/while/body/eval_jaxpr/ptkgd,pkjd->ptkgj/dot_general | solution.py:36
  128.9 0.3 exponential_reduce_fusion.4
  129.3 0.3 convolution_bitcast_fusion.1
  129.6 0.0 copy-done.4
  129.6 0.3 fusion.28
  129.9 6.6 %while.29 = (s32[]{:T(128)}, f32[8,2,4,4,128]{4,3,1,2,0:T(4,128)S(1)}, bf16[8,4,2,512,128]{4,3,1,0,2:T(8,128)(2,1)}, s32[8]{0:T(128)S(1)}, bf16[8,2,4,4,128]{4,3...) while((s32[]{:T(128)}, ...), condition=%wide.region_10.11_spmd, body=%wide.region_9.10_spmd.sunk | while | flops 33917192 | bytes 4531923 | solution.py:86
  129.9 0.1 broadcast_compare_fusion.6
  130.0 3.2 %fusion.57 = f32[8,2,4,4,128]{4,3,1,2,0:T(4,128)S(1)} fusion(f32[8,2,4,4,128]{4,3,1,2,0:T(4,128)S(1)} %get-tuple-element.427, bf16[8,4,2,512,128]{4,3,1,0,2:T(8,128)(2,1)} %get-tuple-element.440, s32[]{:T(128)S(6)} %add.151, s32[]{:T(128)S(6)} %select_n.77, f32[8,2,4,4]{3,1,2,0:T(2,128)S(1)} %get-tuple-element.444, ...), kind=kOutput, calls=%fused_computation.23.clone.1 | convolution fusion | flops 33914880 | bytes 4527616 | tf_op jit(solution)/shard_map/while/body/eval_jaxpr/ptkgj,pkjd->ptkgd/dot_general | solution.py:41
  133.2 0.1 broadcast_compare_fusion.6
  133.3 3.2 %fusion.57 = f32[8,2,4,4,128]{4,3,1,2,0:T(4,128)S(1)} fusion(f32[8,2,4,4,128]{4,3,1,2,0:T(4,128)S(1)} %get-tuple-element.427, bf16[8,4,2,512,128]{4,3,1,0,2:T(8,128)(2,1)} %get-tuple-element.440, s32[]{:T(128)S(6)} %add.151, s32[]{:T(128)S(6)} %select_n.77, f32[8,2,4,4]{3,1,2,0:T(2,128)S(1)} %get-tuple-element.444, ...), kind=kOutput, calls=%fused_computation.23.clone.1 | convolution fusion | flops 33914880 | bytes 4527616 | tf_op jit(solution)/shard_map/while/body/eval_jaxpr/ptkgj,pkjd->ptkgd/dot_general | solution.py:41
  136.5 0.0 copy-start
  136.6 13.7 %fusion.27 = bf16[16,8192]{1,0:T(8,128)(2,1)} fusion(f32[16,8192]{1,0:T(8,128)S(1)} %bitcast.153, bf16[16,128,8192]{2,1,0:T(8,128)(2,1)} %bitcast.151, bf16[16,16,128]{2,1,0:T(8,128)(2,1)S(1)} %bitcast.159), kind=kOutput, calls=%fused_computation.36 | convolution fusion | flops 540934144 | bytes 34406400 | tf_op jit(solution)/shard_map/rbk,bkn->rbn/dot_general | solution.py:91
  150.2 0.0 all-reduce.5.cloned.1.call-update
  150.2 0.0 copy-done
  150.2 0.1 reshape.97
  150.3 22.4 %all-reduce.5.cloned.1.call-done = bf16[16,8192]{1,0:T(8,128)(2,1)} async-done(((bf16[16,8192]{1,0:T(8,128)(2,1)}), bf16[16,8192]{1,0:T(8,128)(2,1)}) %all-reduce.5.cloned.1.call-update) | async-done | bytes 262160 | tf_op jit(solution)/shard_map/psum | solution.py:100
  172.8 1.0 add_convert_fusion
  173.8 0.9 reshape.96
  (20 shorter events, 0.3 us)
Async XLA Ops:
  6.5 115.0 %all-reduce.3.cloned.1.call-start = ((), (), s32[]{:S(2)}) async-start(), calls=%async_computation | async-start | bytes 2097152 | tf_op jit(solution)/shard_map/psum | solution.py:30
  6.5 12.2 %copy-start.6 = (s32[8]{0:T(128)S(1)}, s32[8]{0:T(128)}, u32[]{:S(2)}) copy-start(s32[8]{0:T(128)} %param.16) | copy-start | bytes 100
  6.5 17.2 %copy-start.5 = (s32[8]{0:T(128)S(1)}, s32[8]{0:T(128)}, u32[]{:S(2)}) copy-start(s32[8]{0:T(128)} %param.17) | copy-start | bytes 100
  24.9 7.7 %copy-start.1 = (bf16[8,2,16,128]{3,2,1,0:T(8,128)(2,1)S(1)}, bf16[8,2,16,128]{3,2,1,0:T(8,128)(2,1)}, u32[]{:S(2)}) copy-start(bf16[8,2,16,128]{3,2,1,0:T(8,128)(2,1)} %param.13) | copy-start | bytes 196612
  24.9 7.7 %copy-start.2 = (bf16[8,2,4,2,128]{4,3,2,1,0:T(2,128)(2,1)S(1)}, bf16[8,2,4,2,128]{4,3,2,1,0:T(2,128)(2,1)}, u32[]{:S(2)}) copy-start(bf16[8,2,4,2,128]{4,3,2,1,0:T(2,128)(2,1)} %param.14) | copy-start | bytes 98308
  24.9 7.7 %copy-start.3 = (f32[16,64]{1,0:T(8,128)S(1)}, f32[16,64]{1,0:T(8,128)}, u32[]{:S(2)}) copy-start(f32[16,64]{1,0:T(8,128)} %param.19) | copy-start | bytes 12292
  25.0 147.8 %all-reduce.5.cloned.1.call-start = ((), (), s32[]{:S(2)}) async-start(), calls=%async_computation.1 | async-start | bytes 524288 | tf_op jit(solution)/shard_map/psum | solution.py:100
  123.5 6.0 %copy-start.4 = (bf16[8,4,2,64,128]{4,3,1,0,2:T(8,128)(2,1)S(1)}, bf16[8,4,2,64,128]{4,3,1,0,2:T(8,128)(2,1)}, u32[]{:S(2)}) copy-start(bf16[8,4,2,64,128]{4,3,1,0,2:T(8,128)(2,1)} %all-reduce.3.cloned.1.call-done) | copy-start | bytes 3145732
  136.5 13.7 %copy-start = (bf16[8,2,8192]{2,1,0:T(2,128)(2,1)S(1)}, bf16[8,2,8192]{2,1,0:T(2,128)(2,1)}, u32[]{:S(2)}) copy-start(bf16[8,2,8192]{2,1,0:T(2,128)(2,1)} %param.12) | copy-start | bytes 786436
Sparse Core Ops, SparseCore 0:
  25.0 96.4 all-reduce.2
  150.4 22.3 all-reduce.4
where the time goes:
time: 182 us; the launch traced here: 181 us
  waiting for transfers between devices  110 us (60%)
  matrix products  27.6 us (15%)
  local copies, waits for them, and re-layouts  26.3 us (14%)
  between operations  13.6 us (7%)
  other arithmetic  3.67 us (2%)
    psum x1, waiting for transfers between devices, local(): forked = lax.psum(masked, 'cand').astype(jnp.float32).astype(jnp.bfloat16)  87.6 us
    psum x1, waiting for transfers between devices, local(): totals = lax.psum(term.astype(jnp.bfloat16), 'tp').astype(jnp.float32)  22.4 us
    dot_general x1, matrix products, local(): jnp.einsum('rbk,bkn->rbn', attended.reshape(-1, blocks_here, side), out_v...  13.7 us
    unnamed x17, local copies, waits for them, and re-layouts  12.5 us
    while x1, local copies, waits for them, and re-layouts, local(): peak, total = lax.fori_loop(0, count, first_pass, (peak, total))  7.6 us
    dot_general x4, matrix products, scores_of(): jnp.einsum('ptkgd,pkjd->ptkgj', grouped, keys, preferred_element_type=jnp...  6.99 us
    dot_general x4, matrix products, combine_values(): jnp.einsum('ptkgj,pkjd->ptkgd', weights, values, preferred_element_type=j...  6.96 us
    gather x1, local copies, waits for them, and re-layouts, take_block(): return lax.dynamic_slice_in_dim(cache_row, row_length - BLOCK, BLOCK, 2)  4.99 us
  transfers between devices with their start and end apart: 2, of which 2 were waited for; matrix products, arithmetic and copies ran while one was open for 5% of the time, Pallas kernels for 0%

commit v1 on v0

v1 whole, which is shorter than its diff:
```python
import functools
import math

import jax
import jax.numpy as jnp
from jax import lax
from jax.experimental import pallas as pl
from jax.experimental.pallas import tpu as pltpu
from jax.sharding import PartitionSpec as P

BLOCK = 64
PAD = 16
LOW = -1e30
MESH = pl.DeviceIdType.MESH


def kernel(
    cand_n, tp_n, tile, split,
    lengths, winner, scales, queries, fresh, hidden, cache_hbm, weights_hbm, out,
    cache, weights, first, got, own, near0, up0, far0, down0, mid, near1, up1, far1, down1,
    fork, top_s, sum_s, acc_s, att, lhs, parts,
    cache_sem, weight_sem, send_sem, recv_sem, part_send, part_recv,
):
    me = lax.axis_index("cand")
    tp_me = lax.axis_index("tp")
    problems, kv_here, _, slots, head_dim = cache.shape
    steps_heads = queries.shape[1]
    heads = weights.shape[0] // head_dim
    steps = steps_heads // heads
    group = heads // kv_here
    rows = problems * steps
    half = problems // 2
    hs = kv_here // split
    chunks = half * split
    core = lax.rem(me, 2)
    chip = lax.div(me, 2)
    outer_len = 4
    inner_len = cand_n // 2 // outer_len
    inner_at = lax.rem(chip, inner_len)
    outer_at = lax.div(chip, inner_len)
    sibling = me + 1 - 2 * core

    def ends(at, length, stride):
        low_side = at < length // 2
        step = jnp.where(low_side, stride, -stride)
        has_near = jnp.logical_and(at > 0, at < length - 1)
        crosses = jnp.logical_or(at == length // 2 - 1, at == length // 2)
        return has_near, crosses, me + step, me - step

    inner = ends(inner_at, inner_len, 2)
    outer = ends(outer_at, outer_len, 2 * inner_len)

    barrier = pltpu.get_barrier_semaphore()

    def greet(**where):
        pl.semaphore_signal(barrier, inc=1, device_id=where, device_id_type=MESH)

    greet(cand=sibling)
    count = 1 + (tp_n - 1)
    for has_near, _, far, near in (inner, outer):
        greet(cand=far)

        @pl.when(has_near)
        def _(near=near):
            greet(cand=near)

        count = count + 1 + has_near.astype(jnp.int32)
    for k in range(1, tp_n):
        greet(tp=lax.rem(tp_me + k, tp_n))

    pieces = weight_sem.shape[0]
    piece = weights.shape[0] // pieces

    def cache_copy(p):
        return pltpu.make_async_copy(cache_hbm.at[p], cache.at[p], cache_sem.at[p])

    def weight_copy(i):
        at = pl.ds(i * piece, piece)
        return pltpu.make_async_copy(weights_hbm.at[at], weights.at[at], weight_sem.at[i])

    for p in range(problems):
        cache_copy(p).start()
    for i in range(pieces):
        weight_copy(i).start()
    for p in range(problems):
        cache_copy(p).wait()
    pl.semaphore_wait(barrier, count)

    def remote(src, dst, kind, j, target):
        return pltpu.make_async_remote_copy(
            src_ref=src, dst_ref=dst, send_sem=send_sem.at[kind, j],
            recv_sem=recv_sem.at[kind, j], device_id={"cand": target}, device_id_type=MESH,
        )

    row_i = lax.broadcasted_iota(jnp.int32, (BLOCK, slots), 0)
    col_i = lax.broadcasted_iota(jnp.int32, (BLOCK, slots), 1)

    def extract(p, sub, put):
        shift = jnp.where(winner[p] == me, lengths[p] - BLOCK, 2 * slots)
        pick = (col_i == row_i + shift).astype(jnp.float32).astype(jnp.bfloat16)
        for h in range(hs):
            for kv in range(2):
                put(h, kv, jnp.dot(pick, cache[p, sub * hs + h, kv], preferred_element_type=jnp.float32).astype(jnp.bfloat16))

    def sibling_copy(j):
        return remote(first.at[j], got.at[j], 0, j, sibling)

    def give(j, carry):
        def put(h, kv, value):
            first[j, h, kv] = value

        extract((1 - core) * half + lax.div(j, split), lax.rem(j, split), put)
        sibling_copy(j).start()
        return carry

    lax.fori_loop(0, chunks, give, 0)

    def keep(j, carry):
        def put(h, kv, value):
            own[j, h, kv] = value

        extract(core * half + lax.div(j, split), lax.rem(j, split), put)
        return carry

    lax.fori_loop(0, chunks, keep, 0)

    def make_line(line, kind, base_ref, near_ref, up_ref, far_ref, down_ref):
        has_near, crosses, far_id, near_id = line

        def to_far_in(j):
            return remote(up_ref.at[j], near_ref.at[j], kind, j, far_id)

        def to_far_cross(j):
            return remote(up_ref.at[j], far_ref.at[j], kind + 1, j, far_id)

        def to_near(j):
            return remote(down_ref.at[j], far_ref.at[j], kind + 1, j, near_id)

        def climb(j):
            @pl.when(has_near)
            def _():
                to_far_in(j).wait_recv()
                up_ref[j] = base_ref[j] + near_ref[j]

            @pl.when(jnp.logical_not(has_near))
            def _():
                up_ref[j] = base_ref[j]

            @pl.when(crosses)
            def _():
                to_far_cross(j).start()

            @pl.when(jnp.logical_not(crosses))
            def _():
                to_far_in(j).start()

        def settle(j):
            to_far_cross(j).wait_recv()

            @pl.when(has_near)
            def _():
                down_ref[j] = base_ref[j] + far_ref[j]
                pltpu.make_async_remote_copy(
                    src_ref=down_ref.at[j], dst_ref=far_ref.at[j], send_sem=send_sem.at[kind + 2, j],
                    recv_sem=recv_sem.at[kind + 1, j], device_id={"cand": near_id}, device_id_type=MESH,
                ).start()

            return up_ref[j] + far_ref[j]

        def drain(j):
            @pl.when(crosses)
            def _():
                to_far_cross(j).wait_send()

            @pl.when(jnp.logical_not(crosses))
            def _():
                to_far_in(j).wait_send()

            @pl.when(has_near)
            def _():
                remote(down_ref.at[j], far_ref.at[j], kind + 2, j, near_id).wait_send()

        return climb, settle, drain

    climb0, settle0, drain0 = make_line(inner, 1, own, near0, up0, far0, down0)
    climb1, settle1, drain1 = make_line(outer, 4, mid, near1, up1, far1, down1)

    def loop(body):
        def step(j, carry):
            body(j)
            return carry

        lax.fori_loop(0, chunks, step, 0)

    def enter(j):
        sibling_copy(j).wait_recv()
        own[j] = own[j] + got[j]
        climb0(j)

    loop(enter)

    factor = 1.0 / math.sqrt(head_dim)

    def row_of(width):
        return lax.broadcasted_iota(jnp.int32, (steps_heads, width), 0)

    def col_of(width):
        return lax.broadcasted_iota(jnp.int32, (steps_heads, width), 1)

    def score(q, keys):
        return lax.dot_general(q, keys, (((1,), (1,)), ((), ())), preferred_element_type=jnp.float32) * factor

    def local_part(p):
        q = queries[p]
        s = score(q, cache[p, :, 0].reshape(kv_here * slots, head_dim))
        row, col = row_of(kv_here * slots), col_of(kv_here * slots)
        mine = lax.div(lax.rem(row, heads), group) == lax.div(col, slots)
        s = jnp.where(jnp.logical_and(mine, lax.rem(col, slots) < lengths[p] - BLOCK), s, LOW)
        n = score(q, fresh[p, 0])
        width = fresh.shape[2]
        row, col = row_of(width), col_of(width)
        mine = lax.div(lax.rem(row, heads), group) == lax.div(col, PAD)
        n = jnp.where(jnp.logical_and(mine, lax.rem(col, PAD) <= lax.div(row, heads)), n, LOW)
        top = jnp.maximum(jnp.max(s, 1, keepdims=True), jnp.max(n, 1, keepdims=True))
        s = jnp.exp(s - top)
        n = jnp.exp(n - top)
        top_s[p] = jnp.broadcast_to(top, (steps_heads, head_dim))
        sum_s[p] = jnp.broadcast_to(jnp.sum(s, 1, keepdims=True) + jnp.sum(n, 1, keepdims=True), (steps_heads, head_dim))
        acc_s[p] = jnp.dot(
            s.astype(jnp.bfloat16), cache[p, :, 1].reshape(kv_here * slots, head_dim),
            preferred_element_type=jnp.float32,
        ) + jnp.dot(n.astype(jnp.bfloat16), fresh[p, 1], preferred_element_type=jnp.float32)

    def local_parts(start, stop):
        def step(p, carry):
            local_part(p)
            return carry

        lax.fori_loop(start, stop, step, 0)

    local_parts(0, half)

    def turn(j):
        mid[j] = settle0(j)
        climb1(j)

    loop(turn)
    local_parts(half, problems)

    def fork_copy(j):
        at = core * chunks + j
        return remote(fork.at[at], fork.at[at], 7, j, sibling)

    def finish(j):
        fork[core * chunks + j] = settle1(j)
        fork_copy(j).start()

    loop(finish)

    def closing(j):
        remote(first.at[j], fork.at[(1 - core) * chunks + j], 7, j, sibling).wait_recv()

    loop(closing)

    def fork_part(p, carry):
        q = queries[p]
        both = fork[pl.ds(p * split, split)]
        keys = both[:, :, 0].reshape(kv_here * BLOCK, head_dim)
        values = both[:, :, 1].reshape(kv_here * BLOCK, head_dim)
        s = score(q, keys)
        row, col = row_of(kv_here * BLOCK), col_of(kv_here * BLOCK)
        mine = lax.div(lax.rem(row, heads), group) == lax.div(col, BLOCK)
        s = jnp.where(mine, s, LOW)
        before = top_s[p]
        top = jnp.maximum(before, jnp.max(s, 1, keepdims=True))
        s = jnp.exp(s - top[:, :1])
        scale = jnp.exp(before - top)
        total = sum_s[p] * scale + jnp.sum(s, 1, keepdims=True)
        acc = acc_s[p] * scale + jnp.dot(s.astype(jnp.bfloat16), values, preferred_element_type=jnp.float32)
        att[pl.ds(p * steps_heads, steps_heads), :] = acc / total
        return carry

    lax.fori_loop(0, problems, fork_part, 0)

    pairs = heads // 2
    empty = jnp.zeros((rows, head_dim), jnp.bfloat16)
    for i in range(pairs):
        a = att[pl.ds(2 * i, rows, stride=heads), :].astype(jnp.bfloat16)
        b = att[pl.ds(2 * i + 1, rows, stride=heads), :].astype(jnp.bfloat16)
        lhs[i] = jnp.concatenate(
            [jnp.concatenate([a, empty], 1), jnp.concatenate([empty, b], 1)], 0
        )

    for i in range(pieces):
        weight_copy(i).wait()

    tiles = parts.shape[1]
    per = tile // head_dim

    def part_copy(t, k):
        return pltpu.make_async_remote_copy(
            src_ref=parts.at[tp_me, t], dst_ref=parts.at[tp_me, t], send_sem=part_send.at[k - 1, t],
            recv_sem=part_recv.at[tp_me, t], device_id={"tp": lax.rem(tp_me + k, tp_n)},
            device_id_type=MESH,
        )

    def project(t, carry):
        at = pl.ds(pl.multiple_of(t * tile, tile), tile)
        total = [jnp.zeros((rows, head_dim), jnp.float32) for _ in range(per)]
        for i in range(pairs):
            product = jnp.dot(
                lhs[i], weights[pl.ds(2 * i * head_dim, 2 * head_dim), at], preferred_element_type=jnp.float32
            )
            for c in range(per):
                here = product[:, c * head_dim:(c + 1) * head_dim]
                total[c] = (
                    total[c] + here[:rows] * scales[2 * i, t * per + c]
                    + here[rows:] * scales[2 * i + 1, t * per + c]
                )
        parts[tp_me, t] = jnp.concatenate(total, 1).astype(jnp.bfloat16)
        for k in range(1, tp_n):
            part_copy(t, k).start()
        return carry

    lax.fori_loop(0, tiles, project, 0)

    def gather(t, carry):
        at = pl.ds(pl.multiple_of(t * tile, tile), tile)
        for k in range(1, tp_n):
            source = lax.rem(tp_me + k, tp_n)
            pltpu.make_async_remote_copy(
                src_ref=parts.at[tp_me, t], dst_ref=parts.at[source, t], send_sem=part_send.at[k - 1, t],
                recv_sem=part_recv.at[source, t], device_id={"tp": source}, device_id_type=MESH,
            ).wait_recv()
        total = parts[0, t].astype(jnp.float32)
        for k in range(1, tp_n):
            total = total + parts[k, t].astype(jnp.float32)
        out[:, at] = (hidden[:, at].astype(jnp.float32) + total).astype(jnp.bfloat16)
        return carry

    lax.fori_loop(0, tiles, gather, 0)

    def rest(j):
        sibling_copy(j).wait_send()
        drain0(j)
        drain1(j)
        fork_copy(j).wait_send()

    loop(rest)

    def rest_parts(t, carry):
        for k in range(1, tp_n):
            part_copy(t, k).wait_send()
        return carry

    lax.fori_loop(0, tiles, rest_parts, 0)


def local(cand_n, tp_n, hidden_in, queries, new_kv, kv_cache, lengths, winner, out_values, out_scales):
    problems, kv_here, _, slots, head_dim = kv_cache.shape
    steps, heads = queries.shape[1:3]
    depth, width = out_values.shape
    rows = problems * steps
    split = 2 if kv_here % 2 == 0 else 1
    chunks = problems // 2 * split
    tile = 512
    tiles = width // tile
    flat = queries.reshape(problems, steps * heads, head_dim)
    fresh = jnp.transpose(new_kv, (0, 3, 2, 1, 4))
    fresh = jnp.pad(fresh, ((0, 0), (0, 0), (0, 0), (0, PAD - steps), (0, 0)))
    fresh = fresh.reshape(problems, 2, kv_here * PAD, head_dim)
    smem = pl.BlockSpec(memory_space=pltpu.SMEM)
    vmem = pl.BlockSpec(memory_space=pltpu.VMEM)
    hbm = pl.BlockSpec(memory_space=pl.ANY)
    line = pltpu.VMEM((chunks, kv_here // split, 2, BLOCK, head_dim), jnp.bfloat16)
    stat = pltpu.VMEM((problems, steps * heads, head_dim), jnp.float32)
    dma = pltpu.SemaphoreType.DMA
    out = pl.pallas_call(
        functools.partial(kernel, cand_n, tp_n, tile, split),
        out_shape=jax.ShapeDtypeStruct((rows, width), jnp.bfloat16),
        in_specs=[smem, smem, smem, vmem, vmem, vmem, hbm, hbm],
        out_specs=vmem,
        scratch_shapes=[
            pltpu.VMEM(kv_cache.shape, jnp.bfloat16),
            pltpu.VMEM(out_values.shape, jnp.bfloat16),
            *[line] * 12,
            pltpu.VMEM((problems * split, kv_here // split, 2, BLOCK, head_dim), jnp.bfloat16),
            stat, stat, stat,
            pltpu.VMEM((problems * steps * heads, head_dim), jnp.float32),
            pltpu.VMEM((heads // 2, 2 * rows, 2 * head_dim), jnp.bfloat16),
            pltpu.VMEM((tp_n, tiles, rows, tile), jnp.bfloat16),
            dma((problems,)), dma((8,)), dma((8, chunks)), dma((8, chunks)),
            dma((max(tp_n - 1, 1), tiles)), dma((tp_n, tiles)),
        ],
        compiler_params=pltpu.CompilerParams(
            collective_id=0, has_side_effects=True, vmem_limit_bytes=67043328 - (2 << 20)
        ),
    )(lengths, winner, out_scales, flat, fresh, hidden_in.reshape(rows, width), kv_cache, out_values)
    return out.reshape(hidden_in.shape)


def solution(mesh):
    placed = (
        P("cand", None, None),
        P("cand", None, "tp", None),
        P("cand", None, "tp", None, None),
        P("cand", "tp", None, None, None),
        P("cand"),
        P(),
        P("tp", None),
        P("tp", None),
    )
    return jax.shard_map(
        functools.partial(local, mesh.shape["cand"], mesh.shape["tp"]),
        mesh=mesh, in_specs=placed, out_specs=P("cand", None, None), check_vma=False,
    )
```

time: 182 us -> 71.8 us (0.39)
  waiting for transfers between devices: 110 us -> 0 us
  Pallas kernels: 0 us -> 66.4 us
  matrix products: 27.6 us -> 0 us
  local copies, waits for them, and re-layouts: 26.3 us -> 5.12 us
  between operations: 13.6 us -> 0.01 us
  other arithmetic: 3.67 us -> 0 us
    psum x2 -> x0, waiting for transfers between devices: 110 us -> none  [the longest x1 87.6 us: local(): forked = lax.psum(masked, 'cand').astype(jnp.float32).astype(jnp.bfloat16)]
    pallas_call x0 -> x1, Pallas kernels: none -> 66.4 us  [local(): pl.pallas_call(functools.partial(kernel, cand_n, tp_n, tile, split), out_...]
    dot_general x9 -> x0, matrix products: 27.6 us -> none  [the longest x1 13.7 us: local(): jnp.einsum('rbk,bkn->rbn', attended.reshape(-1, blocks_here, side), out_v...]
    unnamed x17 -> x1, local copies, waits for them, and re-layouts: 12.5 us -> 0.78 us
    while x3 -> x0, local copies, waits for them, and re-layouts: 7.61 us -> none  [the longest x1 7.6 us: local(): peak, total = lax.fori_loop(0, count, first_pass, (peak, total))]
    gather x1 -> x0, local copies, waits for them, and re-layouts: 4.99 us -> none  [take_block(): return lax.dynamic_slice_in_dim(cache_row, row_length - BLOCK, BLOCK, 2)]
    reshape x2, local copies, waits for them, and re-layouts: 0.91 us -> 3.57 us  [the longest x1 1.83 us: local(): return out.reshape(hidden_in.shape)]
  transfers between devices with their start and end apart: 2 -> 0, of which waited for: 2 -> 0; matrix products, arithmetic and copies ran while one was open for 5% -> 0% of each run, Pallas kernels for 0% -> 0%
where the time goes in v1:
time: 71.8 us; the launch traced here: 71.5 us
  Pallas kernels  66.4 us (92%)
  local copies, waits for them, and re-layouts  5.12 us (7%)
    pallas_call x1, Pallas kernels, local(): pl.pallas_call(functools.partial(kernel, cand_n, tp_n, tile, split), out_...  66.4 us
    reshape x1, local copies, waits for them, and re-layouts, local(): return out.reshape(hidden_in.shape)  1.83 us
    reshape x1, local copies, waits for them, and re-layouts, local(): hidden_in.reshape(rows, width)  1.74 us

profile of v1, /device:TPU:0, one launch (start us, length us, event | category | flops | bytes accessed | tf_op | source)
XLA Modules:
  0.0 71.5 jit_solution(8357444351239665909)
XLA Ops:
  0.0 0.8 %copy.10 = bf16[8,2,4,2,128]{4,3,2,1,0:T(2,128)(2,1)S(1)} copy(bf16[8,2,4,2,128]{4,1,2,3,0:T(2,128)(2,1)} %bitcast.5) | data formatting | bytes 65536
  0.8 0.8 %pad.4.clone = bf16[8,2,4,16,128]{4,3,2,1,0:T(8,128)(2,1)} pad(bf16[8,2,4,2,128]{4,3,2,1,0:T(2,128)(2,1)S(1)} %copy.10, bf16[]{:T(256)} %constant.2.clone.1), padding=0_0x0_0x0_0x0_14x0_0 | pad | bytes 294914 | tf_op jit(solution)/shard_map/jit(_pad)/pad | solution.py:370
  1.5 1.7 %reshape.14.hidden = bf16[16,8192]{1,0:T(8,128)(2,1)} reshape(bf16[8,2,8192]{2,1,0:T(2,128)(2,1)} %param.8) | data formatting | bytes 524288 | tf_op jit(solution)/shard_map/reshape | solution.py:398
  3.3 66.4 %shard_map.82 = bf16[16,8192]{1,0:T(8,128)(2,1)} custom-call(s32[8]{0:T(128)} %lengths.1, s32[8]{0:T(128)} %winner.1, f32[16,64]{1,0:T(8,128)} %scales.1, bf16[8,32,128]{2,1,0:T(8,128)(2,1)} %bitcast.4, bf16[8,2,64,128]{3,2,1,0:T(8,128)(2,1)} %bitcast.3, bf16[16,8192]{1,0:T(8,128)(2,1)} %reshape.14.hidden, bf16[8,4,2,512,128]{4,3,2,1,0:T(8,128)(2,1)} %cache_hbm.1, ...), custom_call_target="tpu_custom_call" | custom-call | tf_op jit(solution)/shard_map/pallas_call | solution.py:378
  69.7 1.8 %reshape.15 = bf16[8,2,8192]{2,1,0:T(2,128)(2,1)} reshape(bf16[16,8192]{1,0:T(8,128)(2,1)} %shard_map.82) | data formatting | bytes 524288 | tf_op jit(solution)/shard_map/reshape | solution.py:399

commit v2 on v1

--- a/solution.py
+++ b/solution.py
@@ -9,15 +9,51 @@
 from jax.sharding import PartitionSpec as P
 
 BLOCK = 64
+WINDOW = 128
+LAG = 3
 PAD = 16
 LOW = -1e30
 MESH = pl.DeviceIdType.MESH
 
 
+def pick_kernel(lengths, winner, cache_hbm, blocks, held, sem):
+    problems, kv_here, _, window, _ = held.shape
+    slots = cache_hbm.shape[3]
+    hs = blocks.shape[1]
+    split = kv_here // hs
+    me = lax.axis_index("cand")
+
+    def begin_of(p):
+        begin = lengths[p] - BLOCK
+        base = jnp.clip(lax.div(begin, PAD) * PAD, 0, slots - window)
+        return begin, pl.multiple_of(base, PAD)
+
+    def fetch(p):
+        base = begin_of(p)[1]
+        return pltpu.make_async_copy(
+            cache_hbm.at[p, :, :, pl.ds(base, window), :], held.at[p], sem.at[p]
+        )
+
+    for p in range(problems):
+        fetch(p).start()
+    row = lax.broadcasted_iota(jnp.int32, (BLOCK, window), 0)
+    col = lax.broadcasted_iota(jnp.int32, (BLOCK, window), 1)
+    for p in range(problems):
+        fetch(p).wait()
+        begin, base = begin_of(p)
+        shift = jnp.where(winner[p] == me, begin - base, 4 * window)
+        pick = (col == row + shift).astype(jnp.float32).astype(jnp.bfloat16)
+        for h in range(kv_here):
+            for kv in range(2):
+                blocks[p * split + h // hs, h % hs, kv] = jnp.dot(
+                    pick, held[p, h, kv], preferred_element_type=jnp.float32
+                ).astype(jnp.bfloat16)
+
+
 def kernel(
     cand_n, tp_n, tile, split,
-    lengths, winner, scales, queries, fresh, hidden, cache_hbm, weights_hbm, out,
-    cache, weights, first, got, own, near0, up0, far0, down0, mid, near1, up1, far1, down1,
+    lengths, scales, blocks, queries, fresh, hidden, cache_hbm, weights_hbm, out,
+    cache, weights, got, own, near0, up0, far0, down0, mid, near1, up1, far1, down1,
     fork, top_s, sum_s, acc_s, att, lhs, parts,
     cache_sem, weight_sem, send_sem, recv_sem, part_send, part_recv,
 ):
@@ -80,10 +116,6 @@
 
     for p in range(problems):
         cache_copy(p).start()
-    for i in range(pieces):
-        weight_copy(i).start()
-    for p in range(problems):
-        cache_copy(p).wait()
     pl.semaphore_wait(barrier, count)
 
     def remote(src, dst, kind, j, target):
@@ -92,37 +124,17 @@
             recv_sem=recv_sem.at[kind, j], device_id={"cand": target}, device_id_type=MESH,
         )
 
-    row_i = lax.broadcasted_iota(jnp.int32, (BLOCK, slots), 0)
-    col_i = lax.broadcasted_iota(jnp.int32, (BLOCK, slots), 1)
-
-    def extract(p, sub, put):
-        shift = jnp.where(winner[p] == me, lengths[p] - BLOCK, 2 * slots)
-        pick = (col_i == row_i + shift).astype(jnp.float32).astype(jnp.bfloat16)
-        for h in range(hs):
-            for kv in range(2):
-                put(h, kv, jnp.dot(pick, cache[p, sub * hs + h, kv], preferred_element_type=jnp.float32).astype(jnp.bfloat16))
-
     def sibling_copy(j):
-        return remote(first.at[j], got.at[j], 0, j, sibling)
-
-    def give(j, carry):
-        def put(h, kv, value):
-            first[j, h, kv] = value
-
-        extract((1 - core) * half + lax.div(j, split), lax.rem(j, split), put)
-        sibling_copy(j).start()
-        return carry
-
-    lax.fori_loop(0, chunks, give, 0)
-
-    def keep(j, carry):
-        def put(h, kv, value):
-            own[j, h, kv] = value
-
-        extract(core * half + lax.div(j, split), lax.rem(j, split), put)
-        return carry
-
-    lax.fori_loop(0, chunks, keep, 0)
+        return remote(blocks.at[(1 - core) * chunks + j], got.at[j], 0, j, sibling)
+
+    def loop(body, length):
+        def step(j, carry):
+            body(j)
+            return carry
+
+        lax.fori_loop(0, length, step, 0)
+
+    loop(lambda j: sibling_copy(j).start(), chunks)
 
     def make_line(line, kind, base_ref, near_ref, up_ref, far_ref, down_ref):
         has_near, crosses, far_id, near_id = line
@@ -185,19 +197,14 @@
     climb0, settle0, drain0 = make_line(inner, 1, own, near0, up0, far0, down0)
     climb1, settle1, drain1 = make_line(outer, 4, mid, near1, up1, far1, down1)
 
-    def loop(body):
-        def step(j, carry):
-            body(j)
-            return carry
-
-        lax.fori_loop(0, chunks, step, 0)
-
     def enter(j):
         sibling_copy(j).wait_recv()
-        own[j] = own[j] + got[j]
+        own[j] = blocks[core * chunks + j] + got[j]
         climb0(j)
 
-    loop(enter)
+    loop(enter, chunks)
+    for i in range(pieces):
+        weight_copy(i).start()
 
     factor = 1.0 / math.sqrt(head_dim)
 
@@ -211,6 +218,7 @@
         return lax.dot_general(q, keys, (((1,), (1,)), ((), ())), preferred_element_type=jnp.float32) * factor
 
     def local_part(p):
+        cache_copy(p).wait()
         q = queries[p]
         s = score(q, cache[p, :, 0].reshape(kv_here * slots, head_dim))
         row, col = row_of(kv_here * slots), col_of(kv_here * slots)
@@ -219,8 +227,8 @@
         n = score(q, fresh[p, 0])
         width = fresh.shape[2]
         row, col = row_of(width), col_of(width)
-        mine = lax.div(lax.rem(row, heads), group) == lax.div(col, PAD)
-        n = jnp.where(jnp.logical_and(mine, lax.rem(col, PAD) <= lax.div(row, heads)), n, LOW)
+        mine = lax.div(lax.rem(row, heads), group) == lax.div(col, steps)
+        n = jnp.where(jnp.logical_and(mine, lax.rem(col, steps) <= lax.div(row, heads)), n, LOW)
         top = jnp.maximum(jnp.max(s, 1, keepdims=True), jnp.max(n, 1, keepdims=True))
         s = jnp.exp(s - top)
         n = jnp.exp(n - top)
@@ -231,21 +239,10 @@
             preferred_element_type=jnp.float32,
         ) + jnp.dot(n.astype(jnp.bfloat16), fresh[p, 1], preferred_element_type=jnp.float32)
 
-    def local_parts(start, stop):
-        def step(p, carry):
-            local_part(p)
-            return carry
-
-        lax.fori_loop(start, stop, step, 0)
-
-    local_parts(0, half)
-
     def turn(j):
         mid[j] = settle0(j)
         climb1(j)
 
-    loop(turn)
-    local_parts(half, problems)
 
     def fork_copy(j):
         at = core * chunks + j
@@ -255,12 +252,28 @@
         fork[core * chunks + j] = settle1(j)
         fork_copy(j).start()
 
-    loop(finish)
+    each = pl.cdiv(problems, chunks)
+
+    def advance(j):
+        @pl.when(j < chunks)
+        def _():
+            turn(j)
+
+        for i in range(each):
+            @pl.when(j * each + i < problems)
+            def _(i=i):
+                local_part(j * each + i)
+
+        @pl.when(j >= LAG)
+        def _():
+            finish(j - LAG)
+
+    loop(advance, chunks + LAG)
 
     def closing(j):
-        remote(first.at[j], fork.at[(1 - core) * chunks + j], 7, j, sibling).wait_recv()
-
-    loop(closing)
+        remote(got.at[j], fork.at[(1 - core) * chunks + j], 7, j, sibling).wait_recv()
+
+    loop(closing, chunks)
 
     def fork_part(p, carry):
         q = queries[p]
@@ -335,7 +348,9 @@
         total = parts[0, t].astype(jnp.float32)
         for k in range(1, tp_n):
             total = total + parts[k, t].astype(jnp.float32)
-        out[:, at] = (hidden[:, at].astype(jnp.float32) + total).astype(jnp.bfloat16)
+        for p in range(problems):
+            mixed = hidden[p, :, at].astype(jnp.float32) + total[p * steps:(p + 1) * steps]
+            out[p, :, at] = mixed.astype(jnp.bfloat16)
         return carry
 
     lax.fori_loop(0, tiles, gather, 0)
@@ -346,7 +361,7 @@
         drain1(j)
         fork_copy(j).wait_send()
 
-    loop(rest)
+    loop(rest, chunks)
 
     def rest_parts(t, carry):
         for k in range(1, tp_n):
@@ -367,23 +382,32 @@
     tiles = width // tile
     flat = queries.reshape(problems, steps * heads, head_dim)
     fresh = jnp.transpose(new_kv, (0, 3, 2, 1, 4))
-    fresh = jnp.pad(fresh, ((0, 0), (0, 0), (0, 0), (0, PAD - steps), (0, 0)))
-    fresh = fresh.reshape(problems, 2, kv_here * PAD, head_dim)
+    fresh = fresh.reshape(problems, 2, kv_here * steps, head_dim)
     smem = pl.BlockSpec(memory_space=pltpu.SMEM)
     vmem = pl.BlockSpec(memory_space=pltpu.VMEM)
     hbm = pl.BlockSpec(memory_space=pl.ANY)
     line = pltpu.VMEM((chunks, kv_here // split, 2, BLOCK, head_dim), jnp.bfloat16)
     stat = pltpu.VMEM((problems, steps * heads, head_dim), jnp.float32)
     dma = pltpu.SemaphoreType.DMA
-    out = pl.pallas_call(
+    blocks = pl.pallas_call(
+        pick_kernel,
+        out_shape=jax.ShapeDtypeStruct((problems * split, kv_here // split, 2, BLOCK, head_dim), jnp.bfloat16),
+        in_specs=[smem, smem, hbm],
+        out_specs=vmem,
+        scratch_shapes=[
+            pltpu.VMEM((problems, kv_here, 2, WINDOW, head_dim), jnp.bfloat16), dma((problems,)),
+        ],
+        compiler_params=pltpu.CompilerParams(vmem_limit_bytes=16 << 20),
+    )(lengths, winner, kv_cache)
+    return pl.pallas_call(
         functools.partial(kernel, cand_n, tp_n, tile, split),
-        out_shape=jax.ShapeDtypeStruct((rows, width), jnp.bfloat16),
-        in_specs=[smem, smem, smem, vmem, vmem, vmem, hbm, hbm],
+        out_shape=jax.ShapeDtypeStruct(hidden_in.shape, jnp.bfloat16),
+        in_specs=[smem, smem, vmem, vmem, vmem, vmem, hbm, hbm],
         out_specs=vmem,
         scratch_shapes=[
             pltpu.VMEM(kv_cache.shape, jnp.bfloat16),
             pltpu.VMEM(out_values.shape, jnp.bfloat16),
-            *[line] * 12,
+            *[line] * 11,
             pltpu.VMEM((problems * split, kv_here // split, 2, BLOCK, head_dim), jnp.bfloat16),
             stat, stat, stat,
             pltpu.VMEM((problems * steps * heads, head_dim), jnp.float32),
@@ -395,8 +419,7 @@
         compiler_params=pltpu.CompilerParams(
             collective_id=0, has_side_effects=True, vmem_limit_bytes=67043328 - (2 << 20)
         ),
-    )(lengths, winner, out_scales, flat, fresh, hidden_in.reshape(rows, width), kv_cache, out_values)
-    return out.reshape(hidden_in.shape)
+    )(lengths, out_scales, blocks, flat, fresh, hidden_in, kv_cache, out_values)
 
 
 def solution(mesh):

time: 71.8 us -> 83.2 us (1.16)
  Pallas kernels: 66.4 us -> 74 us
  local copies, waits for them, and re-layouts: 5.12 us -> 8.88 us
    unnamed x1 -> x9, local copies, waits for them, and re-layouts: 0.78 us -> 7.49 us
    pallas_call x1, Pallas kernels: 66.4 us -> 71.5 us  [local(): pl.pallas_call(functools.partial(kernel, cand_n, tp_n, tile, split), out_...]
    reshape x2 -> x0, local copies, waits for them, and re-layouts: 3.57 us -> none  [the longest x1 1.83 us: local(): return out.reshape(hidden_in.shape)]
    pallas_call x0 -> x1, Pallas kernels: none -> 2.5 us  [local(): pl.pallas_call(pick_kernel, out_shape=jax.ShapeDtypeStruct((problems * sp...]
    transpose x0 -> x1, local copies, waits for them, and re-layouts: none -> 1.4 us  [local(): fresh = jnp.transpose(new_kv, (0, 3, 2, 1, 4))]
where the time goes in v2:
time: 83.2 us; the launch traced here: 82.9 us
  Pallas kernels  74 us (89%)
  local copies, waits for them, and re-layouts  8.88 us (11%)
    pallas_call x1, Pallas kernels, local(): pl.pallas_call(functools.partial(kernel, cand_n, tp_n, tile, split), out_...  71.5 us
    unnamed x9, local copies, waits for them, and re-layouts  7.49 us
    pallas_call x1, Pallas kernels, local(): pl.pallas_call(pick_kernel, out_shape=jax.ShapeDtypeStruct((problems * sp...  2.5 us

profile of v2, /device:TPU:0, one launch (start us, length us, event | category | flops | bytes accessed | tf_op | source)
XLA Modules:
  0.0 82.9 jit_solution(5795808146943566442)
XLA Ops:
  0.0 1.4 %copy.9 = bf16[8,2,4,2,128]{4,3,2,1,0:T(2,128)(2,1)} copy(bf16[8,2,4,2,128]{4,1,2,3,0:T(2,128)(2,1)} %bitcast.5) | data formatting | bytes 65536 | tf_op jit(solution)/shard_map/transpose | solution.py:384
  1.4 0.0 copy-start
  1.4 3.4 %copy-done = bf16[8,4,2,512,128]{4,3,2,1,0:T(8,128)(2,1)S(1)} copy-done((bf16[8,4,2,512,128]{4,3,2,1,0:T(8,128)(2,1)S(1)}, bf16[8,4,2,512,128]{4,3,2,1,0:T(8,128)(2,1)}, u32[]{:S(2)}) %copy-start) | copy-done | bytes 8388632
  4.8 0.0 copy-start.2
  4.8 0.7 copy-done.2
  5.4 0.0 copy-start.3
  5.4 0.7 copy-done.3
  6.1 2.5 %shard_map.82.blocks = bf16[16,2,2,64,128]{4,3,2,1,0:T(8,128)(2,1)S(1)} custom-call(s32[8]{0:T(128)S(1)} %copy-done.2, s32[8]{0:T(128)S(1)} %copy-done.3, bf16[8,4,2,512,128]{4,3,2,1,0:T(8,128)(2,1)S(1)} %copy-done), custom_call_target="tpu_custom_call" | custom-call | tf_op jit(solution)/shard_map/pallas_call | solution.py:392
  8.6 0.0 copy-start.1
  8.6 1.0 %copy-done.1 = bf16[16,2,2,64,128]{4,3,2,1,0:T(8,128)(2,1)} copy-done((bf16[16,2,2,64,128]{4,3,2,1,0:T(8,128)(2,1)}, bf16[16,2,2,64,128]{4,3,2,1,0:T(8,128)(2,1)S(1)}, u32[]{:S(2)}) %copy-start.1) | copy-done | bytes 1048600
  9.6 71.5 %shard_map.83 = bf16[8,2,8192]{2,1,0:T(2,128)(2,1)} custom-call(s32[8]{0:T(128)} %lengths.3, f32[16,64]{1,0:T(8,128)} %scales.1, bf16[16,2,2,64,128]{4,3,2,1,0:T(8,128)(2,1)} %copy-done.1, bf16[8,32,128]{2,1,0:T(8,128)(2,1)} %bitcast.4, bf16[8,2,8,128]{3,2,1,0:T(8,128)(2,1)} %bitcast.3, bf16[8,2,8192]{2,1,0:T(2,128)(2,1)} %hidden.1, ...), custom_call_target="tpu_custom_call" | custom-call | tf_op jit(solution)/shard_map/pallas_call | solution.py:402
  81.1 1.8 %copy.11 = bf16[8,2,8192]{2,1,0:T(2,128)(2,1)} copy(bf16[8,2,8192]{2,1,0:T(2,128)(2,1)} %shard_map.83) | data formatting | bytes 524288
Async XLA Ops:
  1.4 3.4 %copy-start = (bf16[8,4,2,512,128]{4,3,2,1,0:T(8,128)(2,1)S(1)}, bf16[8,4,2,512,128]{4,3,2,1,0:T(8,128)(2,1)}, u32[]{:S(2)}) copy-start(bf16[8,4,2,512,128]{4,3,2,1,0:T(8,128)(2,1)} %cache_hbm.3) | copy-start | bytes 25165828
  4.8 0.7 copy-start.2
  5.4 0.7 copy-start.3
  8.6 1.0 %copy-start.1 = (bf16[16,2,2,64,128]{4,3,2,1,0:T(8,128)(2,1)}, bf16[16,2,2,64,128]{4,3,2,1,0:T(8,128)(2,1)S(1)}, u32[]{:S(2)}) copy-start(bf16[16,2,2,64,128]{4,3,2,1,0:T(8,128)(2,1)S(1)} %shard_map.82.blocks) | copy-start | bytes 3145732

commit v3 on v2

--- a/solution.py
+++ b/solution.py
@@ -10,7 +10,7 @@
 
 BLOCK = 64
 WINDOW = 128
-LAG = 3
+LAG = 2
 PAD = 16
 LOW = -1e30
 MESH = pl.DeviceIdType.MESH
@@ -264,11 +264,12 @@
             def _(i=i):
                 local_part(j * each + i)
 
-        @pl.when(j >= LAG)
+        @pl.when(jnp.logical_and(j >= lag, j < chunks + lag))
         def _():
-            finish(j - LAG)
-
-    loop(advance, chunks + LAG)
+            finish(j - lag)
+
+    lag = jnp.where(outer[0], LAG, chunks)
+    loop(advance, 2 * chunks)
 
     def closing(j):
         remote(got.at[j], fork.at[(1 - core) * chunks + j], 7, j, sibling).wait_recv()
@@ -397,7 +398,7 @@
         scratch_shapes=[
             pltpu.VMEM((problems, kv_here, 2, WINDOW, head_dim), jnp.bfloat16), dma((problems,)),
         ],
-        compiler_params=pltpu.CompilerParams(vmem_limit_bytes=16 << 20),
+        compiler_params=pltpu.CompilerParams(vmem_limit_bytes=67043328 - (2 << 20)),
     )(lengths, winner, kv_cache)
     return pl.pallas_call(
         functools.partial(kernel, cand_n, tp_n, tile, split),

time: 83.2 us -> 55.4 us (0.67)
  Pallas kernels: 74 us -> 51.9 us
  local copies, waits for them, and re-layouts: 8.88 us -> 3.23 us
    pallas_call x1, Pallas kernels: 71.5 us -> 47.6 us  [local(): pl.pallas_call(functools.partial(kernel, cand_n, tp_n, tile, split), out_...]
    unnamed x9 -> x1, local copies, waits for them, and re-layouts: 7.49 us -> 1.83 us
    pallas_call x1, Pallas kernels: 2.5 us -> 4.35 us  [local(): pl.pallas_call(pick_kernel, out_shape=jax.ShapeDtypeStruct((problems * sp...]
where the time goes in v3:
time: 55.4 us; the launch traced here: 55.2 us
  Pallas kernels  51.9 us (94%)
  local copies, waits for them, and re-layouts  3.23 us (6%)
    pallas_call x1, Pallas kernels, local(): pl.pallas_call(functools.partial(kernel, cand_n, tp_n, tile, split), out_...  47.6 us
    pallas_call x1, Pallas kernels, local(): pl.pallas_call(pick_kernel, out_shape=jax.ShapeDtypeStruct((problems * sp...  4.35 us
    unnamed x1, local copies, waits for them, and re-layouts  1.83 us
    transpose x1, local copies, waits for them, and re-layouts, local(): fresh = jnp.transpose(new_kv, (0, 3, 2, 1, 4))  1.4 us

profile of v3, /device:TPU:0, one launch (start us, length us, event | category | flops | bytes accessed | tf_op | source)
XLA Modules:
  0.0 55.2 jit_solution(13953805285659173242)
XLA Ops:
  0.0 1.4 %copy.9 = bf16[8,2,4,2,128]{4,3,2,1,0:T(2,128)(2,1)} copy(bf16[8,2,4,2,128]{4,1,2,3,0:T(2,128)(2,1)} %bitcast.5) | data formatting | bytes 65536 | tf_op jit(solution)/shard_map/transpose | solution.py:385
  1.4 4.3 %shard_map.82.blocks = bf16[16,2,2,64,128]{4,3,2,1,0:T(8,128)(2,1)} custom-call(s32[8]{0:T(128)} %lengths.3, s32[8]{0:T(128)} %winner.1, bf16[8,4,2,512,128]{4,3,2,1,0:T(8,128)(2,1)} %cache_hbm.3), custom_call_target="tpu_custom_call" | custom-call | tf_op jit(solution)/shard_map/pallas_call | solution.py:393
  5.8 47.6 %shard_map.83 = bf16[8,2,8192]{2,1,0:T(2,128)(2,1)} custom-call(s32[8]{0:T(128)} %lengths.3, f32[16,64]{1,0:T(8,128)} %scales.1, bf16[16,2,2,64,128]{4,3,2,1,0:T(8,128)(2,1)} %shard_map.82.blocks, bf16[8,32,128]{2,1,0:T(8,128)(2,1)} %bitcast.4, bf16[8,2,8,128]{3,2,1,0:T(8,128)(2,1)} %bitcast.3, bf16[8,2,8192]{2,1,0:T(2,128)(2,1)} %hidden.1, ...), custom_call_target="tpu_custom_call" | custom-call | tf_op jit(solution)/shard_map/pallas_call | solution.py:403
  53.3 1.8 %copy.11 = bf16[8,2,8192]{2,1,0:T(2,128)(2,1)} copy(bf16[8,2,8192]{2,1,0:T(2,128)(2,1)} %shard_map.83) | data formatting | bytes 524288

commit v4 on v3

--- a/solution.py
+++ b/solution.py
@@ -54,8 +54,8 @@
     cand_n, tp_n, tile, split,
     lengths, scales, blocks, queries, fresh, hidden, cache_hbm, weights_hbm, out,
     cache, weights, got, own, near0, up0, far0, down0, mid, near1, up1, far1, down1,
-    fork, top_s, sum_s, acc_s, att, lhs, parts,
-    cache_sem, weight_sem, send_sem, recv_sem, part_send, part_recv,
+    fork, top_s, sum_s, acc_s, att, lhs, parts, other,
+    cache_sem, weight_sem, send_sem, recv_sem, part_send, part_recv, swap_sem, other_send,
 ):
     me = lax.axis_index("cand")
     tp_me = lax.axis_index("tp")
@@ -92,7 +92,7 @@
         pl.semaphore_signal(barrier, inc=1, device_id=where, device_id_type=MESH)
 
     greet(cand=sibling)
-    count = 1 + (tp_n - 1)
+    count = 1 + 2 * (tp_n - 1)
     for has_near, _, far, near in (inner, outer):
         greet(cand=far)
 
@@ -103,6 +103,7 @@
         count = count + 1 + has_near.astype(jnp.int32)
     for k in range(1, tp_n):
         greet(tp=lax.rem(tp_me + k, tp_n))
+        greet(cand=sibling, tp=lax.rem(tp_me + k, tp_n))
 
     pieces = weight_sem.shape[0]
     piece = weights.shape[0] // pieces
@@ -112,7 +113,8 @@
 
     def weight_copy(i):
         at = pl.ds(i * piece, piece)
-        return pltpu.make_async_copy(weights_hbm.at[at], weights.at[at], weight_sem.at[i])
+        columns = pl.ds(pl.multiple_of(core * weights.shape[1], tile), weights.shape[1])
+        return pltpu.make_async_copy(weights_hbm.at[at, columns], weights.at[at], weight_sem.at[i])
 
     for p in range(problems):
         cache_copy(p).start()
@@ -301,51 +303,80 @@
     for i in range(pairs):
         a = att[pl.ds(2 * i, rows, stride=heads), :].astype(jnp.bfloat16)
         b = att[pl.ds(2 * i + 1, rows, stride=heads), :].astype(jnp.bfloat16)
-        lhs[i] = jnp.concatenate(
+        lhs[0, i] = jnp.concatenate(
             [jnp.concatenate([a, empty], 1), jnp.concatenate([empty, b], 1)], 0
         )
 
+    swap = pltpu.make_async_remote_copy(
+        src_ref=lhs.at[0], dst_ref=lhs.at[1], send_sem=swap_sem.at[0], recv_sem=swap_sem.at[1],
+        device_id={"cand": sibling}, device_id_type=MESH,
+    )
+    swap.start()
     for i in range(pieces):
         weight_copy(i).wait()
+    swap.wait_recv()
 
     tiles = parts.shape[1]
+    here_tiles = tiles // 2
     per = tile // head_dim
 
     def part_copy(t, k):
+        at = core * here_tiles + t
         return pltpu.make_async_remote_copy(
-            src_ref=parts.at[tp_me, t], dst_ref=parts.at[tp_me, t], send_sem=part_send.at[k - 1, t],
-            recv_sem=part_recv.at[tp_me, t], device_id={"tp": lax.rem(tp_me + k, tp_n)},
+            src_ref=parts.at[tp_me, at], dst_ref=parts.at[tp_me, at], send_sem=part_send.at[k - 1, t],
+            recv_sem=part_recv.at[tp_me, at], device_id={"tp": lax.rem(tp_me + k, tp_n)},
             device_id_type=MESH,
         )
 
+    def other_copy(t, k):
+        at = core * here_tiles + t
+        return pltpu.make_async_remote_copy(
+            src_ref=other.at[t], dst_ref=parts.at[tp_me, at], send_sem=other_send.at[k, t],
+            recv_sem=part_recv.at[tp_me, at],
+            device_id={"cand": sibling, "tp": lax.rem(tp_me + k, tp_n)}, device_id_type=MESH,
+        )
+
     def project(t, carry):
         at = pl.ds(pl.multiple_of(t * tile, tile), tile)
-        total = [jnp.zeros((rows, head_dim), jnp.float32) for _ in range(per)]
+        first_scale = (core * here_tiles + t) * per
+        total = [jnp.zeros((2, rows, head_dim), jnp.float32) for _ in range(per)]
         for i in range(pairs):
             product = jnp.dot(
-                lhs[i], weights[pl.ds(2 * i * head_dim, 2 * head_dim), at], preferred_element_type=jnp.float32
+                lhs[:, i].reshape(4 * rows, 2 * head_dim),
+                weights[pl.ds(2 * i * head_dim, 2 * head_dim), at], preferred_element_type=jnp.float32,
             )
             for c in range(per):
-                here = product[:, c * head_dim:(c + 1) * head_dim]
+                here = product[:, c * head_dim:(c + 1) * head_dim].reshape(2, 2, rows, head_dim)
                 total[c] = (
-                    total[c] + here[:rows] * scales[2 * i, t * per + c]
-                    + here[rows:] * scales[2 * i + 1, t * per + c]
+                    total[c] + here[:, 0] * scales[2 * i, first_scale + c]
+                    + here[:, 1] * scales[2 * i + 1, first_scale + c]
                 )
-        parts[tp_me, t] = jnp.concatenate(total, 1).astype(jnp.bfloat16)
+        whole = jnp.concatenate(total, 2).astype(jnp.bfloat16)
+        parts[tp_me, core * here_tiles + t] = whole[0]
+        other[t] = whole[1]
         for k in range(1, tp_n):
+            other_copy(t, k).start()
             part_copy(t, k).start()
+        other_copy(t, 0).start()
         return carry
 
-    lax.fori_loop(0, tiles, project, 0)
+    lax.fori_loop(0, here_tiles, project, 0)
 
     def gather(t, carry):
         at = pl.ds(pl.multiple_of(t * tile, tile), tile)
+
+        def arrived(source):
+            pltpu.make_async_remote_copy(
+                src_ref=other.at[0], dst_ref=parts.at[source, t], send_sem=swap_sem.at[0],
+                recv_sem=part_recv.at[source, t], device_id={"cand": sibling}, device_id_type=MESH,
+            ).wait_recv()
+
+        @pl.when(lax.div(t, here_tiles) != core)
+        def _():
+            arrived(tp_me)
+
         for k in range(1, tp_n):
-            source = lax.rem(tp_me + k, tp_n)
-            pltpu.make_async_remote_copy(
-                src_ref=parts.at[tp_me, t], dst_ref=parts.at[source, t], send_sem=part_send.at[k - 1, t],
-                recv_sem=part_recv.at[source, t], device_id={"tp": source}, device_id_type=MESH,
-            ).wait_recv()
+            arrived(lax.rem(tp_me + k, tp_n))
         total = parts[0, t].astype(jnp.float32)
         for k in range(1, tp_n):
             total = total + parts[k, t].astype(jnp.float32)
@@ -355,6 +386,7 @@
         return carry
 
     lax.fori_loop(0, tiles, gather, 0)
+    swap.wait_send()
 
     def rest(j):
         sibling_copy(j).wait_send()
@@ -365,11 +397,13 @@
     loop(rest, chunks)
 
     def rest_parts(t, carry):
+        other_copy(t, 0).wait_send()
         for k in range(1, tp_n):
             part_copy(t, k).wait_send()
+            other_copy(t, k).wait_send()
         return carry
 
-    lax.fori_loop(0, tiles, rest_parts, 0)
+    lax.fori_loop(0, here_tiles, rest_parts, 0)
 
 
 def local(cand_n, tp_n, hidden_in, queries, new_kv, kv_cache, lengths, winner, out_values, out_scales):
@@ -407,15 +441,17 @@
         out_specs=vmem,
         scratch_shapes=[
             pltpu.VMEM(kv_cache.shape, jnp.bfloat16),
-            pltpu.VMEM(out_values.shape, jnp.bfloat16),
+            pltpu.VMEM((depth, width // 2), jnp.bfloat16),
             *[line] * 11,
             pltpu.VMEM((problems * split, kv_here // split, 2, BLOCK, head_dim), jnp.bfloat16),
             stat, stat, stat,
             pltpu.VMEM((problems * steps * heads, head_dim), jnp.float32),
-            pltpu.VMEM((heads // 2, 2 * rows, 2 * head_dim), jnp.bfloat16),
+            pltpu.VMEM((2, heads // 2, 2 * rows, 2 * head_dim), jnp.bfloat16),
             pltpu.VMEM((tp_n, tiles, rows, tile), jnp.bfloat16),
+            pltpu.VMEM((tiles // 2, rows, tile), jnp.bfloat16),
             dma((problems,)), dma((8,)), dma((8, chunks)), dma((8, chunks)),
-            dma((max(tp_n - 1, 1), tiles)), dma((tp_n, tiles)),
+            dma((max(tp_n - 1, 1), tiles // 2)), dma((tp_n, tiles)),
+            dma((2,)), dma((tp_n, tiles // 2)),
         ],
         compiler_params=pltpu.CompilerParams(
             collective_id=0, has_side_effects=True, vmem_limit_bytes=67043328 - (2 << 20)

time: 55.4 us -> 55 us (level)
  no operation moved by 1% of the time
where the time goes in v4:
time: 55 us; the launch traced here: 54.7 us
  Pallas kernels  51.5 us (94%)
  local copies, waits for them, and re-layouts  3.23 us (6%)
    pallas_call x1, Pallas kernels, local(): pl.pallas_call(functools.partial(kernel, cand_n, tp_n, tile, split), out_...  47.1 us
    pallas_call x1, Pallas kernels, local(): pl.pallas_call(pick_kernel, out_shape=jax.ShapeDtypeStruct((problems * sp...  4.35 us
    unnamed x1, local copies, waits for them, and re-layouts  1.83 us
    transpose x1, local copies, waits for them, and re-layouts, local(): fresh = jnp.transpose(new_kv, (0, 3, 2, 1, 4))  1.4 us

profile of v4, /device:TPU:0, one launch (start us, length us, event | category | flops | bytes accessed | tf_op | source)
XLA Modules:
  0.0 54.7 jit_solution(5115254775833551147)
XLA Ops:
  0.0 1.4 %copy.9 = bf16[8,2,4,2,128]{4,3,2,1,0:T(2,128)(2,1)} copy(bf16[8,2,4,2,128]{4,1,2,3,0:T(2,128)(2,1)} %bitcast.5) | data formatting | bytes 65536 | tf_op jit(solution)/shard_map/transpose | solution.py:419
  1.4 4.3 %shard_map.82.blocks = bf16[16,2,2,64,128]{4,3,2,1,0:T(8,128)(2,1)} custom-call(s32[8]{0:T(128)} %lengths.3, s32[8]{0:T(128)} %winner.1, bf16[8,4,2,512,128]{4,3,2,1,0:T(8,128)(2,1)} %cache_hbm.3), custom_call_target="tpu_custom_call" | custom-call | tf_op jit(solution)/shard_map/pallas_call | solution.py:427
  5.8 47.1 %shard_map.83 = bf16[8,2,8192]{2,1,0:T(2,128)(2,1)} custom-call(s32[8]{0:T(128)} %lengths.3, f32[16,64]{1,0:T(8,128)} %scales.1, bf16[16,2,2,64,128]{4,3,2,1,0:T(8,128)(2,1)} %shard_map.82.blocks, bf16[8,32,128]{2,1,0:T(8,128)(2,1)} %bitcast.4, bf16[8,2,8,128]{3,2,1,0:T(8,128)(2,1)} %bitcast.3, bf16[8,2,8192]{2,1,0:T(2,128)(2,1)} %hidden.1, ...), custom_call_target="tpu_custom_call" | custom-call | tf_op jit(solution)/shard_map/pallas_call | solution.py:437
  52.9 1.8 %copy.11 = bf16[8,2,8192]{2,1,0:T(2,128)(2,1)} copy(bf16[8,2,8192]{2,1,0:T(2,128)(2,1)} %shard_map.83) | data formatting | bytes 524288
